TPU v7x, 256 devices: a whole 4x4x8 slice. The times are simulated.
256 devices in a mesh: energy: 128 (over z_lo, x, y, core), mom: 2 (over z_hi).
Axes of the slice: x: 4, y: 4, z: 8 (z_hi: 2, z_lo: 4; z = z_hi * 4 + z_lo), core: 2. Of those that a mesh axis runs over, the one named last changes fastest.
Arguments:
- system_matrix: float32 [2, 128, 4, 384, 384], P(None, 'energy', 'mom'), may hold values from -1 to 5
- approx_inverse: float32 [2, 128, 4, 384], P(None, 'energy', 'mom'), may hold values from -1.2 to 1.2
- mode_weight: float32 [4, 6], replicated, may hold values from 0.05 to 0.3
- phonon_shift: int32 [4, 6], replicated, may hold values from -8 to 8
- pairing: int32 [4, 4], replicated, may hold values from 0 to 3
- coupling: float32 [384, 384], P('energy'), may hold values from 0.3 to 1.5
- energy_weight: float32 [128], P('energy'), may hold values from 0.5 to 2
- force_weight: float32 [384, 384], P('energy'), may hold values from -0.25 to 0.25
Outputs:
- green: float32 [2, 128, 4, 384, 384], P(None, 'energy', 'mom')
- sigma: float32 [2, 128, 4, 384, 384], P(None, 'energy', 'mom')
- force: float32 [384, 384], P('energy')
All inputs are finite; a program needn't handle non-finite values.
Results may differ from a plain program's by a relative error of at most 0.0001.
Values sent between devices are 32-bit elements; how exact they have to be, the bound alone decides.
A program may use at most 128 MiB of HBM per device.

v0:
```python
import functools

import jax
import jax.numpy as jnp
from jax import lax
from jax.experimental import pallas as pl
from jax.experimental.pallas import tpu as pltpu
from jax.sharding import Mesh
from jax.sharding import PartitionSpec as P

AXES = ("zl", "x", "y", "c", "zh")
ENERGY = ("zl", "x", "y", "c")
MESH_ID = pl.DeviceIdType.MESH
F32 = jnp.float32
BF16 = jnp.bfloat16
B = 384
T = 3
VMEM = pl.BlockSpec(memory_space=pltpu.VMEM)
SMEM = pl.BlockSpec(memory_space=pltpu.SMEM)


def split(x):
    hi = x.astype(BF16)
    lo = (x - hi.astype(F32)).astype(BF16)
    return hi, lo


def put_left(ref, real, imag, row):
    rows = pl.ds(row, B)
    for col, part in ((0, real), (B, imag)):
        hi, lo = split(part)
        ref[rows, pl.ds(col, B)] = hi
        ref[rows, pl.ds(2 * B + col, B)] = hi
        ref[rows, pl.ds(4 * B + col, B)] = lo


def put_right(ref, real, imag):
    rh, rl = split(real)
    ih, il = split(imag)
    for base, r, i in ((0, rh, ih), (2 * B, rl, il), (4 * B, rh, ih)):
        ref[pl.ds(base, B), pl.ds(0, B)] = r
        ref[pl.ds(base, B), pl.ds(B, B)] = i
        ref[pl.ds(base + B, B), pl.ds(0, B)] = -i
        ref[pl.ds(base + B, B), pl.ds(B, B)] = r


def newton_kernel(m_ref, c_ref, g_ref, lin_ref, left, right, xr, xi):
    k = pl.program_id(0)
    row = lax.broadcasted_iota(jnp.int32, (B, B), 0)
    col = lax.broadcasted_iota(jnp.int32, (B, B), 1)
    eye = row == col
    one = jnp.where(eye, 1.0, 0.0).astype(F32)
    cr = c_ref[0, pl.ds(k, 1), :]
    ci = c_ref[1, pl.ds(k, 1), :]
    cr_col = jnp.sum(jnp.where(eye, cr, 0.0), axis=1, keepdims=True)
    ci_col = jnp.sum(jnp.where(eye, ci, 0.0), axis=1, keepdims=True)
    mr = m_ref[0, 0, 0]
    mi = m_ref[1, 0, 0]
    yr = one - (mr * cr - mi * ci)
    yi = -(mr * ci + mi * cr)
    put_left(left, yr, yi, 0)
    put_right(right, yr, yi)
    ar = one + yr
    xr[...] = cr_col * ar - ci_col * yi
    xi[...] = cr_col * yi + ci_col * ar
    y0 = jnp.dot(left[pl.ds(0, B), :], right[...], preferred_element_type=F32)
    put_left(left, y0[:, :B], y0[:, B:], B)
    put_left(left, xr[...], xi[...], 0)
    put_right(right, y0[:, :B], y0[:, B:])
    both = jnp.dot(left[...], right[...], preferred_element_type=F32)
    x1r = xr[...] + both[:B, :B]
    x1i = xi[...] + both[:B, B:]
    xr[...] = x1r
    xi[...] = x1i
    put_left(left, x1r, x1i, 0)
    put_right(right, both[B:, :B], both[B:, B:])
    last = jnp.dot(left[pl.ds(0, B), :], right[...], preferred_element_type=F32)
    for part, (ref, off) in enumerate(((xr, 0), (xi, B))):
        out = ref[...] + last[:, off : off + B]
        g_ref[part, 0, 0] = out
        for t in range(T):
            lin_ref[0, t, part] = out[:, 128 * t : 128 * (t + 1)]


def newton(matrix, approx):
    return pl.pallas_call(
        newton_kernel,
        grid=(2,),
        out_shape=(
            jax.ShapeDtypeStruct((2, 1, 2, B, B), F32),
            jax.ShapeDtypeStruct((2, T, 2, B, 128), F32),
        ),
        in_specs=[
            pl.BlockSpec((2, 1, 1, B, B), lambda k: (0, 0, k, 0, 0)),
            pl.BlockSpec((2, 2, B), lambda k: (0, 0, 0)),
        ],
        out_specs=(
            pl.BlockSpec((2, 1, 1, B, B), lambda k: (0, 0, k, 0, 0)),
            pl.BlockSpec((1, T, 2, B, 128), lambda k: (k, 0, 0, 0, 0)),
        ),
        scratch_shapes=[
            pltpu.VMEM((2 * B, 6 * B), BF16),
            pltpu.VMEM((6 * B, 2 * B), BF16),
            pltpu.VMEM((B, B), F32),
            pltpu.VMEM((B, B), F32),
        ],
        compiler_params=pltpu.CompilerParams(vmem_limit_bytes=40 << 20),
        name="newton",
    )(matrix, approx)


def here():
    return {a: lax.axis_index(a) for a in AXES}


def ring_z(me, d):
    z = lax.rem(me["zh"] * 4 + me["zl"] + d, 8)
    return z, (lax.rem(z, 4), me["x"], me["y"], me["c"], z // 4)


def plane(me, i):
    x = lax.rem(me["x"] + i // 8, 4)
    y = lax.rem(me["y"] + lax.rem(i // 2, 4), 4)
    c = lax.rem(me["c"] + lax.rem(i, 2), 2)
    return (x * 4 + y) * 2 + c, (me["zl"], x, y, c, me["zh"])


def greet(me):
    barrier = pltpu.get_barrier_semaphore()

    def along_z(d, carry):
        pl.semaphore_signal(barrier, inc=1, device_id=ring_z(me, d)[1], device_id_type=MESH_ID)
        return carry

    def in_plane(i, carry):
        pl.semaphore_signal(barrier, inc=1, device_id=plane(me, i)[1], device_id_type=MESH_ID)
        return carry

    lax.fori_loop(1, 8, along_z, 0)
    lax.fori_loop(1, 32, in_plane, 0)
    pl.semaphore_wait(barrier, 38)


def send(src, dst, ssem, rsem, device):
    pltpu.make_async_remote_copy(
        src_ref=src, dst_ref=dst, send_sem=ssem, recv_sem=rsem, device_id=device, device_id_type=MESH_ID
    ).start()


def wait_for(ref, sem):
    pltpu.make_async_copy(ref, ref, sem).wait()


def exchange_kernel(
    lin, weight, shift, pairing, coupling, out,
    zb, pb, cb, rb, kmat, shifted, xs,
    zs, zr, ps, pr, bs, br, ws, wr,
):
    me = here()
    my_z = me["zh"] * 4 + me["zl"]
    my_p = (me["x"] * 4 + me["y"]) * 2 + me["c"]
    mine = pl.ds(3 * my_p, 3)
    greet(me)

    for k in range(2):
        for t in range(T):

            def along_z(d, carry, k=k, t=t):
                z, device = ring_z(me, d)
                rows = pl.ds(pl.multiple_of(96 * lax.rem(z, 4), 8), 96)
                send(lin.at[k, t, z // 4, rows], zb.at[k, t, my_z], zs.at[k, t], zr.at[k, t], device)
                return carry

            lax.fori_loop(1, 8, along_z, 0)
            rows = pl.ds(pl.multiple_of(96 * me["zl"], 8), 96)
            pltpu.make_async_copy(lin.at[k, t, me["zh"], rows], zb.at[k, t, my_z], zr.at[k, t]).start()

    e = lax.broadcasted_iota(jnp.int32, (128, 128), 0)
    f = lax.broadcasted_iota(jnp.int32, (128, 128), 1)
    for q in range(4):
        total = jnp.zeros((128, 128), F32)
        for m in range(6):
            total = total + jnp.where(f == e - shift[q, m], weight[q, m], 0.0)
        shifted[q] = total
    for kk in range(4):
        for ll in range(4):
            block = jnp.zeros((128, 128), F32)
            for q in range(4):
                same = (e * 0 + pairing[kk, q]) == ll
                block = block + jnp.where(same, shifted[q], 0.0)
            hi, lo = split(block)
            row = pl.ds(128 * ((kk % 2) * 2 + kk // 2), 128)
            col = 128 * ((ll % 2) * 2 + ll // 2)
            kmat[row, pl.ds(col, 128)] = hi
            kmat[row, pl.ds(512 + col, 128)] = hi
            kmat[row, pl.ds(1024 + col, 128)] = lo

    def plane_forward(k, ts, slot):
        def in_plane(i, carry):
            p, device = plane(me, i)
            send(zb.at[k, ts, :, pl.ds(3 * p, 3)], pb.at[k, ts, :, mine], ps.at[slot], pr.at[slot], device)
            return carry

        lax.fori_loop(1, 32, in_plane, 0)
        pltpu.make_async_copy(zb.at[k, ts, :, mine], pb.at[k, ts, :, mine], pr.at[slot]).start()

    def plane_back(t):
        def in_plane(i, carry):
            p, device = plane(me, i)
            send(cb.at[t, :, :, pl.ds(3 * p, 3)], rb.at[t, :, :, mine], bs.at[t], br.at[t], device)
            return carry

        lax.fori_loop(1, 32, in_plane, 0)
        pltpu.make_async_copy(cb.at[t, :, :, mine], rb.at[t, :, :, mine], br.at[t]).start()

    def z_back(t):
        wait_for(rb.at[t], br.at[t])
        rows = pl.ds(pl.multiple_of(96 * me["zl"], 8), 96)
        for k in range(2):

            def along_z(d, carry, k=k):
                z, device = ring_z(me, d)
                send(rb.at[t, k, z], out.at[t, k, me["zh"], rows], ws.at[t], wr.at[t], device)
                return carry

            lax.fori_loop(1, 8, along_z, 0)
            pltpu.make_async_copy(rb.at[t, k, my_z], out.at[t, k, me["zh"], rows], wr.at[t]).start()

    def convolve(t):
        for k in range(2):
            for z in range(8):
                rows = pl.ds(256 * k + 32 * z, 32)
                for j in range(3):
                    hi, lo = split(pb[k, t, z, pl.ds(j, 32, stride=3), :])
                    cols = pl.ds(128 * j, 128)
                    xs[rows, cols] = hi
                    xs[pl.ds(512 + 256 * k + 32 * z, 32), cols] = lo
                    xs[pl.ds(1024 + 256 * k + 32 * z, 32), cols] = hi
        result = jnp.dot(kmat[...], xs[...], preferred_element_type=F32)
        for j in range(3):
            scaled = result[:, 128 * j : 128 * (j + 1)] * coupling[pl.ds(j, 1), pl.ds(128 * t, 128)]
            for k in range(2):
                for z in range(8):
                    start = 256 * k + 32 * z
                    cb[t, k, z, pl.ds(j, 32, stride=3), :] = scaled[start : start + 32, :]

    for t in range(T):
        wait_for(zb.at[0, t], zr.at[0, t])
    plane_forward(0, pl.ds(0, T), 0)
    for t in range(T):
        wait_for(zb.at[1, t], zr.at[1, t])
        plane_forward(1, pl.ds(t, 1), 1 + t)
        if t == 0:
            wait_for(pb.at[0], pr.at[0])
        if t == 2:
            z_back(0)
        wait_for(pb.at[1, t], pr.at[1 + t])
        convolve(t)
        plane_back(t)
    z_back(1)
    z_back(2)

    for t in range(T):
        wait_for(out.at[t], wr.at[t])
    for k in range(2):
        for t in range(T):
            wait_for(zb.at[k, t, pl.ds(0, 7)], zs.at[k, t])
    wait_for(pb.at[0, :, :, pl.ds(0, 93)], ps.at[0])
    for t in range(T):
        wait_for(pb.at[1, pl.ds(t, 1), :, pl.ds(0, 93)], ps.at[1 + t])
        wait_for(rb.at[t, :, :, pl.ds(0, 93)], bs.at[t])
        wait_for(rb.at[t, :, pl.ds(0, 7)], ws.at[t])


def exchange(lin, weight, shift, pairing, coupling):
    dma = pltpu.SemaphoreType.DMA
    return pl.pallas_call(
        exchange_kernel,
        out_shape=jax.ShapeDtypeStruct((T, 2, 2, B, 128), F32),
        in_specs=[VMEM, SMEM, SMEM, SMEM, VMEM],
        out_specs=VMEM,
        scratch_shapes=[
            pltpu.VMEM((2, T, 8, 96, 128), F32),
            pltpu.VMEM((2, T, 8, 96, 128), F32),
            pltpu.VMEM((T, 2, 8, 96, 128), F32),
            pltpu.VMEM((T, 2, 8, 96, 128), F32),
            pltpu.VMEM((512, 1536), BF16),
            pltpu.VMEM((4, 128, 128), F32),
            pltpu.VMEM((1536, 384), BF16),
            dma((2, T)), dma((2, T)),
            dma((4,)), dma((4,)),
            dma((T,)), dma((T,)),
            dma((T,)), dma((T,)),
        ],
        compiler_params=pltpu.CompilerParams(
            collective_id=1, has_side_effects=True, vmem_limit_bytes=48 << 20
        ),
        name="exchange",
    )(lin, weight, shift, pairing, coupling)


def force_kernel(g_ref, s_ref, w_ref, sigma_ref, f_ref, left, right):
    for n in range(4):
        part, k = n // 2, n % 2
        hi, lo = split(g_ref[part, 0, k])
        for base, value in ((0, hi), (4 * B, hi), (8 * B, lo)):
            left[:, pl.ds(base + n * B, B)] = value
        for t in range(T):
            s = s_ref[t, k, part]
            sigma_ref[part, 0, k, :, pl.ds(128 * t, 128)] = s
            hi, lo = split(s if part == 0 else -s)
            for base, value in ((0, hi), (4 * B, lo), (8 * B, hi)):
                right[pl.ds(base + n * B, B), pl.ds(128 * t, 128)] = value
    total = jnp.dot(left[...], right[...], preferred_element_type=F32) * w_ref[0]
    for t in range(T):
        f_ref[t] = total[:, 128 * t : 128 * (t + 1)]


def sigma_and_force(green, raw, energy_weight):
    return pl.pallas_call(
        force_kernel,
        out_shape=(
            jax.ShapeDtypeStruct((2, 1, 2, B, B), F32),
            jax.ShapeDtypeStruct((T, B, 128), F32),
        ),
        in_specs=[VMEM, VMEM, SMEM],
        out_specs=(VMEM, VMEM),
        scratch_shapes=[
            pltpu.VMEM((B, 12 * B), BF16),
            pltpu.VMEM((12 * B, B), BF16),
        ],
        compiler_params=pltpu.CompilerParams(vmem_limit_bytes=48 << 20),
        name="sigma_force",
    )(green, raw, energy_weight)


def reduce_kernel(f, fw, out, near, own, far, ns, nr, fs, fr):
    me = here()
    my_z = me["zh"] * 4 + me["zl"]
    my_p = (me["x"] * 4 + me["y"]) * 2 + me["c"]
    greet(me)

    def in_plane(i, carry):
        p, device = plane(me, i)
        send(f.at[:, :, pl.ds(3 * p, 3)], near.at[my_p], ns, nr, device)
        return carry

    lax.fori_loop(1, 32, in_plane, 0)
    pltpu.make_async_copy(f.at[:, :, pl.ds(3 * my_p, 3)], near.at[my_p], nr).start()
    wait_for(near, nr)
    total = near[0]
    for p in range(1, 32):
        total = total + near[p]
    own[...] = total

    def along_z(d, carry):
        z, device = ring_z(me, d)
        send(own.at[:, lax.rem(z, 4)], far.at[my_z], fs, fr, device)
        return carry

    lax.fori_loop(1, 8, along_z, 0)
    pltpu.make_async_copy(own.at[:, me["zl"]], far.at[my_z], fr).start()
    wait_for(far, fr)
    total = far[0]
    for z in range(1, 8):
        total = total + far[z]
    for t in range(T):
        out[:, pl.ds(128 * t, 128)] = total[t] * fw[:, pl.ds(128 * t, 128)]
    wait_for(near.at[pl.ds(0, 31)], ns)
    wait_for(far.at[pl.ds(0, 7)], fs)


def reduce_force(partial, force_weight):
    dma = pltpu.SemaphoreType.DMA
    return pl.pallas_call(
        reduce_kernel,
        out_shape=jax.ShapeDtypeStruct((3, B), F32),
        in_specs=[VMEM, VMEM],
        out_specs=VMEM,
        scratch_shapes=[
            pltpu.VMEM((32, T, 4, 3, 128), F32),
            pltpu.VMEM((T, 4, 3, 128), F32),
            pltpu.VMEM((8, T, 3, 128), F32),
            dma, dma, dma, dma,
        ],
        compiler_params=pltpu.CompilerParams(collective_id=2, has_side_effects=True),
        name="reduce_force",
    )(partial.reshape(T, 4, 96, 128), force_weight)


def per_device(
    system_matrix, approx_inverse, mode_weight, phonon_shift, pairing, coupling, energy_weight, force_weight
):
    green, lin = newton(system_matrix, approx_inverse.reshape(2, 2, B))
    raw = exchange(lin, mode_weight, phonon_shift, pairing, coupling)
    sigma, partial = sigma_and_force(green, raw, energy_weight)
    force = reduce_force(partial, force_weight)
    return green, sigma, force


def solution(mesh):
    torus = Mesh(mesh.devices.reshape(4, 4, 4, 2, 2), AXES)
    return jax.shard_map(
        per_device,
        mesh=torus,
        in_specs=(
            P(None, ENERGY, "zh", None, None),
            P(None, ENERGY, "zh", None),
            P(),
            P(),
            P(),
            P(ENERGY, None),
            P(ENERGY),
            P(ENERGY, None),
        ),
        out_specs=(
            P(None, ENERGY, "zh", None, None),
            P(None, ENERGY, "zh", None, None),
            P(ENERGY, None),
        ),
        check_vma=False,
    )
```

profile of v0, /device:TPU:1, one launch (start us, length us, event | category | flops | bytes accessed | tf_op | source)
XLA Modules:
  0.0 182.2 jit_solution(9872195613981643867)
XLA Ops:
  0.6 0.0 copy-start.5
  1.3 0.0 copy-start
  1.3 1.7 copy-done
  3.0 0.0 copy-start.3
  3.0 0.7 copy-done.3
  3.7 0.0 copy-start.4
  3.7 0.0 copy-start.6
  3.7 0.0 copy-start.7
  3.7 17.6 %newton.1 = (f32[2,1,2,384,384]{4,3,2,1,0:T(8,128)}, f32[2,3,2,384,128]{4,3,2,1,0:T(8,128)S(1)}) custom-call(f32[2,1,2,384,384]{4,3,2,1,0:T(8,128)S(1)} %copy-done, f32[2,2,384]{2,1,0:T(2,128)S(1)} %bitcast.3), custom_call_target="tpu_custom_call" | custom-call | tf_op jit(solution)/shard_map/newton/pallas_call | solution.py:86
  21.3 0.0 copy-done.5
  21.3 0.0 copy-done.4
  21.3 0.0 copy-done.6
  21.3 0.0 copy-done.7
  21.3 0.0 copy-start.1
  21.3 134.8 %exchange.1.s_ref = f32[3,2,2,384,128]{4,3,2,1,0:T(8,128)S(1)} custom-call(f32[2,3,2,384,128]{4,3,2,1,0:T(8,128)S(1)} %get-tuple-element.8.lin, f32[4,6]{1,0:T(4,128)S(1)} %copy-done.5, s32[4,6]{1,0:T(4,128)S(1)} %copy-done.6, s32[4,4]{1,0:T(4,128)S(1)} %copy-done.7, f32[3,384]{1,0:T(4,128)S(1)} %copy-done.4), custom_call_target="tpu_custom_call" | custom-call | tf_op jit(solution)/shard_map/exchange/pallas_call | solution.py:277
  156.1 0.0 copy-done.1
  156.2 2.5 %sigma_force.1 = (f32[2,1,2,384,384]{4,3,2,1,0:T(8,128)}, f32[3,384,128]{2,1,0:T(8,128)S(1)}) custom-call(f32[2,1,2,384,384]{4,3,2,1,0:T(8,128)S(1)} %copy-done.1, f32[3,2,2,384,128]{4,3,2,1,0:T(8,128)S(1)} %exchange.1.s_ref, f32[1]{0:T(128)S(6)} %copy.12.w_ref), custom_call_target="tpu_custom_call" | custom-call | tf_op jit(solution)/shard_map/sigma_force/pallas_call | solution.py:320
  158.6 0.0 copy-start.2
  158.6 0.8 copy-done.2
  159.5 21.5 %reduce_force.1 = f32[3,384]{1,0:T(4,128)} custom-call(f32[3,4,96,128]{3,2,1,0:T(8,128)} %bitcast.2, f32[3,384]{1,0:T(4,128)} %fw.1), custom_call_target="tpu_custom_call" | custom-call | tf_op jit(solution)/shard_map/reduce_force/pallas_call | solution.py:375
  180.9 1.3 copy.13
Async XLA Ops:
  0.6 20.7 %copy-start.5 = (f32[4,6]{1,0:T(4,128)S(1)}, f32[4,6]{1,0:T(4,128)}, u32[]{:S(2)}) copy-start(f32[4,6]{1,0:T(4,128)} %weight.1) | copy-start | bytes 292
  1.3 1.7 copy-start
  3.0 0.7 copy-start.3
  3.7 17.6 %copy-start.4 = (f32[3,384]{1,0:T(4,128)S(1)}, f32[3,384]{1,0:T(4,128)}, u32[]{:S(2)}) copy-start(f32[3,384]{1,0:T(4,128)} %coupling.1) | copy-start | bytes 13828
  3.7 17.7 %copy-start.6 = (s32[4,6]{1,0:T(4,128)S(1)}, s32[4,6]{1,0:T(4,128)}, u32[]{:S(2)}) copy-start(s32[4,6]{1,0:T(4,128)} %shift.1) | copy-start | bytes 292
  3.7 17.7 %copy-start.7 = (s32[4,4]{1,0:T(4,128)S(1)}, s32[4,4]{1,0:T(4,128)}, u32[]{:S(2)}) copy-start(s32[4,4]{1,0:T(4,128)} %pairing.1) | copy-start | bytes 196
  21.3 134.8 %copy-start.1 = (f32[2,1,2,384,384]{4,3,2,1,0:T(8,128)S(1)}, f32[2,1,2,384,384]{4,3,2,1,0:T(8,128)}, u32[]{:S(2)}) copy-start(f32[2,1,2,384,384]{4,3,2,1,0:T(8,128)} %get-tuple-element.14.g_ref) | copy-start | bytes 7077892
  158.6 0.8 copy-start.2
where the time goes:
time: 182 us
  Pallas kernels  176 us (97%)
  local copies, waits for them, and re-layouts  4.47 us (2%)
    pallas_call x1, Pallas kernels, exchange(): pl.pallas_call(exchange_kernel, out_shape=jax.ShapeDtypeStruct((T, 2, 2,...  135 us
    pallas_call x1, Pallas kernels, reduce_force(): pl.pallas_call(reduce_kernel, out_shape=jax.ShapeDtypeStruct((3, B), F32)...  21.5 us
    pallas_call x1, Pallas kernels, newton(): pl.pallas_call(newton_kernel, grid=(2,), out_shape=(jax.ShapeDtypeStruct(...  17.6 us
    unnamed x17, local copies, waits for them, and re-layouts  4.47 us

commit v1 on v0

v1 whole, which is shorter than its diff:
```python
import functools

import jax
import jax.numpy as jnp
from jax import lax
from jax.experimental import pallas as pl
from jax.experimental.pallas import tpu as pltpu
from jax.sharding import Mesh
from jax.sharding import PartitionSpec as P

AXES = ("zl", "x", "y", "c", "zh")
ENERGY = ("zl", "x", "y", "c")
MESH_ID = pl.DeviceIdType.MESH
F32 = jnp.float32
BF16 = jnp.bfloat16
B = 384
T = 3
VMEM = pl.BlockSpec(memory_space=pltpu.VMEM)
SMEM = pl.BlockSpec(memory_space=pltpu.SMEM)


def split(x):
    hi = x.astype(BF16)
    lo = (x - hi.astype(F32)).astype(BF16)
    return hi, lo


def put_left(ref, real, imag, row):
    rows = pl.ds(row, B)
    for col, part in ((0, real), (B, imag)):
        hi, lo = split(part)
        ref[rows, pl.ds(col, B)] = hi
        ref[rows, pl.ds(2 * B + col, B)] = hi
        ref[rows, pl.ds(4 * B + col, B)] = lo


def put_right(ref, real, imag):
    rh, rl = split(real)
    ih, il = split(imag)
    for base, r, i in ((0, rh, ih), (2 * B, rl, il), (4 * B, rh, ih)):
        for t in range(T):
            cut = slice(128 * t, 128 * (t + 1))
            ref[pl.ds(base, B), pl.ds(256 * t, 128)] = r[:, cut]
            ref[pl.ds(base, B), pl.ds(256 * t + 128, 128)] = i[:, cut]
            ref[pl.ds(base + B, B), pl.ds(256 * t, 128)] = -i[:, cut]
            ref[pl.ds(base + B, B), pl.ds(256 * t + 128, 128)] = r[:, cut]


def parts_of(wide):
    real = jnp.concatenate([wide[:, 256 * t : 256 * t + 128] for t in range(T)], axis=1)
    imag = jnp.concatenate([wide[:, 256 * t + 128 : 256 * t + 256] for t in range(T)], axis=1)
    return real, imag


def newton_but_last(k, matrix, approx, left, right, xr, xi):
    row = lax.broadcasted_iota(jnp.int32, (B, B), 0)
    col = lax.broadcasted_iota(jnp.int32, (B, B), 1)
    eye = row == col
    one = jnp.where(eye, 1.0, 0.0).astype(F32)
    cr = approx[0, pl.ds(k, 1), :]
    ci = approx[1, pl.ds(k, 1), :]
    cr_col = jnp.sum(jnp.where(eye, cr, 0.0), axis=1, keepdims=True)
    ci_col = jnp.sum(jnp.where(eye, ci, 0.0), axis=1, keepdims=True)
    mr = matrix[k, 0]
    mi = matrix[k, 1]
    yr = one - (mr * cr - mi * ci)
    yi = -(mr * ci + mi * cr)
    put_left(left, yr, yi, 0)
    put_right(right, yr, yi)
    ar = one + yr
    xr[...] = cr_col * ar - ci_col * yi
    xi[...] = cr_col * yi + ci_col * ar
    y0 = jnp.dot(left[pl.ds(0, B), :], right[...], preferred_element_type=F32)
    y0r, y0i = parts_of(y0)
    put_left(left, y0r, y0i, B)
    put_left(left, xr[...], xi[...], 0)
    put_right(right, y0r, y0i)
    both = jnp.dot(left[...], right[...], preferred_element_type=F32)
    dr, di = parts_of(both[:B])
    y1r, y1i = parts_of(both[B:])
    x1r = xr[...] + dr
    x1i = xi[...] + di
    xr[...] = x1r
    xi[...] = x1i
    put_left(left, x1r, x1i, 0)
    put_right(right, y1r, y1i)


def newton_last(k, t, left, right, xr, xi, lin):
    last = jnp.dot(left[pl.ds(0, B), :], right[:, pl.ds(256 * t, 256)], preferred_element_type=F32)
    cols = pl.ds(128 * t, 128)
    lin[k, t, 0] = xr[:, cols] + last[:, :128]
    lin[k, t, 1] = xi[:, cols] + last[:, 128:]


def here():
    return {a: lax.axis_index(a) for a in AXES}


def ring_z(me, d):
    z = lax.rem(me["zh"] * 4 + me["zl"] + d, 8)
    return z, (lax.rem(z, 4), me["x"], me["y"], me["c"], z // 4)


def plane(me, i):
    x = lax.rem(me["x"] + i // 8, 4)
    y = lax.rem(me["y"] + lax.rem(i // 2, 4), 4)
    c = lax.rem(me["c"] + lax.rem(i, 2), 2)
    return (x * 4 + y) * 2 + c, (me["zl"], x, y, c, me["zh"])


def greet(me):
    barrier = pltpu.get_barrier_semaphore()

    def along_z(d, carry):
        pl.semaphore_signal(barrier, inc=1, device_id=ring_z(me, d)[1], device_id_type=MESH_ID)
        return carry

    def in_plane(i, carry):
        pl.semaphore_signal(barrier, inc=1, device_id=plane(me, i)[1], device_id_type=MESH_ID)
        return carry

    lax.fori_loop(1, 8, along_z, 0)
    lax.fori_loop(1, 32, in_plane, 0)
    return barrier


def send(src, dst, ssem, rsem, device):
    pltpu.make_async_remote_copy(
        src_ref=src, dst_ref=dst, send_sem=ssem, recv_sem=rsem, device_id=device, device_id_type=MESH_ID
    ).start()


def wait_for(ref, sem):
    pltpu.make_async_copy(ref, ref, sem).wait()


def step_kernel(
    matrix_hbm, approx, weight, shift, pairing, coupling, energy_weight, force_weight,
    out, lin, force,
    matrix, left, right, xr, xi, zb, pb, cb, rb, kmat, shifted, xs, fleft, fright, fb, near, own, far,
    ms, zs, zr, ps, pr, bs, br, ws, wr, ns, nr, fs, fr,
):
    me = here()
    my_z = me["zh"] * 4 + me["zl"]
    my_p = (me["x"] * 4 + me["y"]) * 2 + me["c"]
    mine = pl.ds(3 * my_p, 3)
    my_rows = pl.ds(pl.multiple_of(96 * me["zl"], 8), 96)

    loads = [pltpu.make_async_copy(matrix_hbm.at[:, 0, k], matrix.at[k], ms.at[k]) for k in range(2)]
    for load in loads:
        load.start()
    barrier = greet(me)

    def z_forward(k, t):
        def along_z(d, carry):
            z, device = ring_z(me, d)
            rows = pl.ds(pl.multiple_of(96 * lax.rem(z, 4), 8), 96)
            send(lin.at[k, t, z // 4, rows], zb.at[k, t, my_z], zs.at[k, t], zr.at[k, t], device)
            return carry

        lax.fori_loop(1, 8, along_z, 0)
        pltpu.make_async_copy(lin.at[k, t, me["zh"], my_rows], zb.at[k, t, my_z], zr.at[k, t]).start()

    def plane_forward(k, t):
        wait_for(zb.at[k, t], zr.at[k, t])

        def in_plane(i, carry):
            p, device = plane(me, i)
            send(zb.at[k, t, :, pl.ds(3 * p, 3)], pb.at[k, t, :, mine], ps.at[k, t], pr.at[k, t], device)
            return carry

        lax.fori_loop(1, 32, in_plane, 0)
        pltpu.make_async_copy(zb.at[k, t, :, mine], pb.at[k, t, :, mine], pr.at[k, t]).start()

    def plane_back(k, t):
        def in_plane(i, carry):
            p, device = plane(me, i)
            send(cb.at[t, k, :, pl.ds(3 * p, 3)], rb.at[t, k, :, mine], bs.at[t, k], br.at[t, k], device)
            return carry

        lax.fori_loop(1, 32, in_plane, 0)
        pltpu.make_async_copy(cb.at[t, k, :, mine], rb.at[t, k, :, mine], br.at[t, k]).start()

    def z_back(k, t):
        wait_for(rb.at[t, k], br.at[t, k])

        def along_z(d, carry):
            z, device = ring_z(me, d)
            send(rb.at[t, k, z], out.at[t, k, me["zh"], my_rows], ws.at[t, k], wr.at[t, k], device)
            return carry

        lax.fori_loop(1, 8, along_z, 0)
        pltpu.make_async_copy(rb.at[t, k, my_z], out.at[t, k, me["zh"], my_rows], wr.at[t, k]).start()

    def build_kernel():
        e = lax.broadcasted_iota(jnp.int32, (128, 128), 0)
        f = lax.broadcasted_iota(jnp.int32, (128, 128), 1)
        for q in range(4):
            total = jnp.zeros((128, 128), F32)
            for m in range(6):
                total = total + jnp.where(f == e - shift[q, m], weight[q, m], 0.0)
            shifted[q] = total
        for kk in range(4):
            for ll in range(4):
                block = jnp.zeros((128, 128), F32)
                for q in range(4):
                    same = (e * 0 + pairing[kk, q]) == ll
                    block = block + jnp.where(same, shifted[q], 0.0)
                hi, lo = split(block)
                row = pl.ds(128 * ((kk % 2) * 2 + kk // 2), 128)
                col = 128 * ((ll % 2) * 2 + ll // 2)
                kmat[row, pl.ds(col, 128)] = hi
                kmat[row, pl.ds(512 + col, 128)] = hi
                kmat[row, pl.ds(1024 + col, 128)] = lo

    def convolve(t):
        for k in range(2):
            wait_for(pb.at[k, t], pr.at[k, t])
            for z in range(8):
                rows = pl.ds(256 * k + 32 * z, 32)
                for j in range(3):
                    hi, lo = split(pb[k, t, z, pl.ds(j, 32, stride=3), :])
                    cols = pl.ds(128 * j, 128)
                    xs[rows, cols] = hi
                    xs[pl.ds(512 + 256 * k + 32 * z, 32), cols] = lo
                    xs[pl.ds(1024 + 256 * k + 32 * z, 32), cols] = hi
        for k in range(2):
            result = jnp.dot(kmat[pl.ds(256 * k, 256), :], xs[...], preferred_element_type=F32)
            for j in range(3):
                scaled = result[:, 128 * j : 128 * (j + 1)] * coupling[pl.ds(j, 1), pl.ds(128 * t, 128)]
                for z in range(8):
                    cb[t, k, z, pl.ds(j, 32, stride=3), :] = scaled[32 * z : 32 * z + 32, :]
            plane_back(k, t)

    def build_force_left():
        for n in range(4):
            part, k = n // 2, n % 2
            for t in range(T):
                hi, lo = split(lin[k, t, part])
                for base, value in ((0, hi), (4 * B, hi), (8 * B, lo)):
                    fleft[:, pl.ds(base + n * B + 128 * t, 128)] = value

    def force_part(t):
        for k in range(2):
            wait_for(out.at[t, k], wr.at[t, k])
            for part in range(2):
                s = out[t, k, part]
                n = 2 * part + k
                hi, lo = split(s if part == 0 else -s)
                for base, value in ((0, hi), (4 * B, lo), (8 * B, hi)):
                    fright[pl.ds(base + n * B, B), :] = value
        total = jnp.dot(fleft[...], fright[...], preferred_element_type=F32) * energy_weight[0]
        for z in range(4):
            fb[t, z] = total[96 * z : 96 * (z + 1), :]

        def in_plane(i, carry):
            p, device = plane(me, i)
            send(fb.at[t, :, pl.ds(3 * p, 3)], near.at[t, my_p], ns.at[t], nr.at[t], device)
            return carry

        lax.fori_loop(1, 32, in_plane, 0)
        pltpu.make_async_copy(fb.at[t, :, mine], near.at[t, my_p], nr.at[t]).start()

    def force_along_z(t):
        wait_for(near.at[t], nr.at[t])
        total = near[t, 0]
        for p in range(1, 32):
            total = total + near[t, p]
        own[t] = total

        def along_z(d, carry):
            z, device = ring_z(me, d)
            send(own.at[t, lax.rem(z, 4)], far.at[t, my_z], fs.at[t], fr.at[t], device)
            return carry

        lax.fori_loop(1, 8, along_z, 0)
        pltpu.make_async_copy(own.at[t, me["zl"]], far.at[t, my_z], fr.at[t]).start()

    def force_out(t):
        wait_for(far.at[t], fr.at[t])
        total = far[t, 0]
        for z in range(1, 8):
            total = total + far[t, z]
        cols = pl.ds(128 * t, 128)
        force[:, cols] = total * force_weight[:, cols]

    loads[0].wait()
    newton_but_last(0, matrix, approx, left, right, xr, xi)
    pl.semaphore_wait(barrier, 38)
    for t in range(T):
        newton_last(0, t, left, right, xr, xi, lin)
        if t < 2:
            z_forward(0, t)
    loads[1].wait()
    newton_but_last(1, matrix, approx, left, right, xr, xi)
    for t in range(T):
        newton_last(1, t, left, right, xr, xi, lin)
        if t < 2:
            z_forward(1, t)
    z_forward(0, 2)
    z_forward(1, 2)
    plane_forward(0, 0)
    build_kernel()
    plane_forward(0, 1)
    plane_forward(1, 0)
    convolve(0)
    plane_forward(1, 1)
    convolve(1)
    plane_forward(0, 2)
    z_back(0, 0)
    z_back(1, 0)
    build_force_left()
    plane_forward(1, 2)
    z_back(0, 1)
    z_back(1, 1)
    convolve(2)
    z_back(0, 2)
    z_back(1, 2)
    force_part(0)
    force_part(1)
    force_along_z(0)
    force_along_z(1)
    force_part(2)
    force_along_z(2)
    for t in range(T):
        force_out(t)

    for t in range(T):
        for k in range(2):
            wait_for(zb.at[k, t, pl.ds(0, 7)], zs.at[k, t])
            wait_for(pb.at[k, t, :, pl.ds(0, 93)], ps.at[k, t])
            wait_for(rb.at[t, k, :, pl.ds(0, 93)], bs.at[t, k])
            wait_for(rb.at[t, k, pl.ds(0, 7)], ws.at[t, k])
        wait_for(near.at[t, pl.ds(0, 31)], ns.at[t])
        wait_for(far.at[t, pl.ds(0, 7)], fs.at[t])


def step(matrix, approx, weight, shift, pairing, coupling, energy_weight, force_weight):
    dma = pltpu.SemaphoreType.DMA
    return pl.pallas_call(
        step_kernel,
        out_shape=(
            jax.ShapeDtypeStruct((T, 2, 2, B, 128), F32),
            jax.ShapeDtypeStruct((2, T, 2, B, 128), F32),
            jax.ShapeDtypeStruct((3, B), F32),
        ),
        in_specs=[pl.BlockSpec(memory_space=pl.ANY), VMEM, SMEM, SMEM, SMEM, VMEM, SMEM, VMEM],
        out_specs=(VMEM, VMEM, VMEM),
        scratch_shapes=[
            pltpu.VMEM((2, 2, B, B), F32),
            pltpu.VMEM((2 * B, 6 * B), BF16),
            pltpu.VMEM((6 * B, 2 * B), BF16),
            pltpu.VMEM((B, B), F32),
            pltpu.VMEM((B, B), F32),
            pltpu.VMEM((2, T, 8, 96, 128), F32),
            pltpu.VMEM((2, T, 8, 96, 128), F32),
            pltpu.VMEM((T, 2, 8, 96, 128), F32),
            pltpu.VMEM((T, 2, 8, 96, 128), F32),
            pltpu.VMEM((512, 1536), BF16),
            pltpu.VMEM((4, 128, 128), F32),
            pltpu.VMEM((1536, 384), BF16),
            pltpu.VMEM((B, 12 * B), BF16),
            pltpu.VMEM((12 * B, 128), BF16),
            pltpu.VMEM((T, 4, 96, 128), F32),
            pltpu.VMEM((T, 32, 4, 3, 128), F32),
            pltpu.VMEM((T, 4, 3, 128), F32),
            pltpu.VMEM((T, 8, 3, 128), F32),
            dma((2,)),
            dma((2, T)), dma((2, T)),
            dma((2, T)), dma((2, T)),
            dma((T, 2)), dma((T, 2)),
            dma((T, 2)), dma((T, 2)),
            dma((T,)), dma((T,)),
            dma((T,)), dma((T,)),
        ],
        compiler_params=pltpu.CompilerParams(
            collective_id=1, has_side_effects=True, vmem_limit_bytes=52 << 20
        ),
        name="step",
    )(matrix, approx, weight, shift, pairing, coupling, energy_weight, force_weight)


def layout_kernel(raw, lin, f_in, green, sigma, f_out):
    part = pl.program_id(0)
    k = pl.program_id(1)
    for t in range(T):
        cols = pl.ds(128 * t, 128)
        green[0, 0, 0, :, cols] = lin[k, t, part]
        sigma[0, 0, 0, :, cols] = raw[t, k, part]
    f_out[...] = f_in[...]


def final_layouts(raw, lin, force):
    block = pl.BlockSpec((1, 1, 1, B, B), lambda part, k: (part, 0, k, 0, 0))
    return pl.pallas_call(
        layout_kernel,
        grid=(2, 2),
        out_shape=(
            jax.ShapeDtypeStruct((2, 1, 2, B, B), F32),
            jax.ShapeDtypeStruct((2, 1, 2, B, B), F32),
            jax.ShapeDtypeStruct((3, B), F32),
        ),
        in_specs=[VMEM, VMEM, VMEM],
        out_specs=(block, block, pl.BlockSpec((3, B), lambda part, k: (0, 0))),
        name="layouts",
    )(raw, lin, force)


def per_device(
    system_matrix, approx_inverse, mode_weight, phonon_shift, pairing, coupling, energy_weight, force_weight
):
    raw, lin, force = step(
        system_matrix, approx_inverse.reshape(2, 2, B), mode_weight, phonon_shift, pairing, coupling,
        energy_weight, force_weight,
    )
    return final_layouts(raw, lin, force)


def solution(mesh):
    torus = Mesh(mesh.devices.reshape(4, 4, 4, 2, 2), AXES)
    return jax.shard_map(
        per_device,
        mesh=torus,
        in_specs=(
            P(None, ENERGY, "zh", None, None),
            P(None, ENERGY, "zh", None),
            P(),
            P(),
            P(),
            P(ENERGY, None),
            P(ENERGY),
            P(ENERGY, None),
        ),
        out_specs=(
            P(None, ENERGY, "zh", None, None),
            P(None, ENERGY, "zh", None, None),
            P(ENERGY, None),
        ),
        check_vma=False,
    )
```

time: 182 us -> 154 us (0.85)
  Pallas kernels: 176 us -> 148 us
    pallas_call x4 -> x2, Pallas kernels: 176 us -> 148 us  [the longest x1 143 us: step(): pl.pallas_call(step_kernel, out_shape=(jax.ShapeDtypeStruct((T, 2, 2, B,...]
    unnamed x17 -> x14, local copies, waits for them, and re-layouts: 4.47 us -> 4.7 us
where the time goes in v1:
time: 154 us
  Pallas kernels  148 us (96%)
  local copies, waits for them, and re-layouts  4.7 us (3%)
    pallas_call x1, Pallas kernels, step(): pl.pallas_call(step_kernel, out_shape=(jax.ShapeDtypeStruct((T, 2, 2, B,...  143 us
    pallas_call x1, Pallas kernels, final_layouts(): pl.pallas_call(layout_kernel, grid=(2, 2), out_shape=(jax.ShapeDtypeStruc...  4.94 us
    unnamed x14, local copies, waits for them, and re-layouts  4.7 us

profile of v1, /device:TPU:1, one launch (start us, length us, event | category | flops | bytes accessed | tf_op | source)
XLA Modules:
  0.0 153.7 jit_solution(7902043599354171032)
XLA Ops:
  1.3 0.0 copy-start.1
  1.3 0.7 copy-done.1
  2.0 0.0 copy-start.2
  2.0 0.7 copy-done.2
  2.7 0.0 copy-start.3
  2.7 0.7 copy-done.3
  3.4 0.0 copy-start.4
  3.4 0.7 copy-done.4
  4.0 0.0 copy-start.5
  4.0 0.7 copy-done.5
  4.7 0.0 copy-start.6
  4.7 0.7 copy-done.6
  5.4 142.7 %step.1 = (f32[3,2,2,384,128]{4,3,2,1,0:T(8,128)}, f32[2,3,2,384,128]{4,3,2,1,0:T(8,128)}, f32[3,384]{1,0:T(4,128)S(1)}) custom-call(f32[2,1,2,384,384]{4,3,2,1,0:T(8,128)} %matrix_hbm.1, f32[2,2,384]{2,1,0:T(2,128)S(1)} %bitcast.1, f32[4,6]{1,0:T(4,128)S(1)} %copy-done.4, s32[4,6]{1,0:T(4,128)S(1)} %copy-done.5, s32[4,4]{1,0:T(4,128)S(1)} %copy-done.6, ...), custom_call_target="tpu_custom_call" | custom-call | tf_op jit(solution)/shard_map/step/pallas_call | solution.py:341
  148.1 0.0 copy-start
  148.1 0.6 copy-done
  148.7 4.9 %layouts.1 = (f32[2,1,2,384,384]{4,3,2,1,0:T(8,128)}, f32[2,1,2,384,384]{4,3,2,1,0:T(8,128)}, f32[3,384]{1,0:T(4,128)}) custom-call(f32[3,2,2,384,128]{4,3,2,1,0:T(8,128)} %get-tuple-element.6.raw, f32[2,3,2,384,128]{4,3,2,1,0:T(8,128)} %get-tuple-element.7.lin, f32[3,384]{1,0:T(4,128)} %copy-done), custom_call_target="tpu_custom_call" | custom-call | tf_op jit(solution)/shard_map/layouts/pallas_call | solution.py:396
Async XLA Ops:
  1.3 0.7 copy-start.1
  2.0 0.7 copy-start.2
  2.7 0.7 copy-start.3
  3.4 0.7 copy-start.4
  4.0 0.7 copy-start.5
  4.7 0.7 copy-start.6
  148.1 0.6 copy-start

commit v2 on v1

--- a/solution.py
+++ b/solution.py
@@ -136,10 +136,11 @@
 
 
 def step_kernel(
-    matrix_hbm, approx, weight, shift, pairing, coupling, energy_weight, force_weight,
-    out, lin, force,
-    matrix, left, right, xr, xi, zb, pb, cb, rb, kmat, shifted, xs, fleft, fright, fb, near, own, far,
-    ms, zs, zr, ps, pr, bs, br, ws, wr, ns, nr, fs, fr,
+    matrix_hbm, approx_hbm, weight_hbm, shift_hbm, pairing_hbm, coupling_hbm, energy_hbm, force_hbm,
+    green_hbm, sigma_hbm, force,
+    approx, weight, shift, pairing, coupling, energy_weight, force_weight, small_sem, lin, out,
+    matrix, left, right, xr, xi, zb, pb, cb, rb, kmat, shifted, xs, fleft, fright, fa, fb, near, own, far,
+    ms, zs, zr, ps, pr, bs, br, ws, wr, ns, nr, fs, fr, gs, ss,
 ):
     me = here()
     my_z = me["zh"] * 4 + me["zl"]
@@ -148,9 +149,31 @@
     my_rows = pl.ds(pl.multiple_of(96 * me["zl"], 8), 96)
 
     loads = [pltpu.make_async_copy(matrix_hbm.at[:, 0, k], matrix.at[k], ms.at[k]) for k in range(2)]
-    for load in loads:
+    small = [
+        pltpu.make_async_copy(src, dst, small_sem.at[n])
+        for n, (src, dst) in enumerate(
+            (
+                (approx_hbm, approx),
+                (weight_hbm, weight),
+                (shift_hbm, shift),
+                (pairing_hbm, pairing),
+                (coupling_hbm, coupling),
+                (energy_hbm, energy_weight),
+                (force_hbm, force_weight),
+            )
+        )
+    ]
+    for load in small + loads:
         load.start()
     barrier = greet(me)
+
+    def green_out(k, t, part):
+        place = green_hbm.at[part, 0, k, :, pl.ds(128 * t, 128)]
+        return pltpu.make_async_copy(lin.at[k, t, part], place, gs.at[k, t, part])
+
+    def sigma_out(k, t, part):
+        place = sigma_hbm.at[part, 0, k, :, pl.ds(128 * t, 128)]
+        return pltpu.make_async_copy(out.at[t, k, part], place, ss.at[k, t, part])
 
     def z_forward(k, t):
         def along_z(d, carry):
@@ -234,86 +257,97 @@
             plane_back(k, t)
 
     def build_force_left():
-        for n in range(4):
-            part, k = n // 2, n % 2
-            for t in range(T):
-                hi, lo = split(lin[k, t, part])
-                for base, value in ((0, hi), (4 * B, hi), (8 * B, lo)):
-                    fleft[:, pl.ds(base + n * B + 128 * t, 128)] = value
+        for k in range(2):
+            for part in range(2):
+                for t in range(T):
+                    hi, lo = split(lin[k, t, part])
+                    for term, value in ((0, hi), (1, hi), (2, lo)):
+                        fleft[k, :, pl.ds((2 * term + part) * B + 128 * t, 128)] = value
+
+    def force_term(t, k):
+        wait_for(out.at[t, k], wr.at[t, k])
+        for part in range(2):
+            sigma_out(k, t, part).start()
+            s = out[t, k, part]
+            hi, lo = split(s if part == 0 else -s)
+            for term, value in ((0, hi), (1, lo), (2, hi)):
+                fright[pl.ds((2 * term + part) * B, B), :] = value
+        return jnp.dot(fleft[k], fright[...], preferred_element_type=F32)
 
     def force_part(t):
-        for k in range(2):
-            wait_for(out.at[t, k], wr.at[t, k])
-            for part in range(2):
-                s = out[t, k, part]
-                n = 2 * part + k
-                hi, lo = split(s if part == 0 else -s)
-                for base, value in ((0, hi), (4 * B, lo), (8 * B, hi)):
-                    fright[pl.ds(base + n * B, B), :] = value
-        total = jnp.dot(fleft[...], fright[...], preferred_element_type=F32) * energy_weight[0]
+        fa[...] = force_term(t, 0)
+        fa[...] = (fa[...] + force_term(t, 1)) * energy_weight[0]
         for z in range(4):
-            fb[t, z] = total[96 * z : 96 * (z + 1), :]
+            for j in range(3):
+                fb[t, pl.ds(3 * z + j, 32, stride=12), :] = fa[pl.ds(96 * z + j, 32, stride=3), :]
 
         def in_plane(i, carry):
             p, device = plane(me, i)
-            send(fb.at[t, :, pl.ds(3 * p, 3)], near.at[t, my_p], ns.at[t], nr.at[t], device)
+            send(fb.at[t, pl.ds(12 * p, 12)], near.at[t, pl.ds(12 * my_p, 12)], ns.at[t], nr.at[t], device)
             return carry
 
         lax.fori_loop(1, 32, in_plane, 0)
-        pltpu.make_async_copy(fb.at[t, :, mine], near.at[t, my_p], nr.at[t]).start()
+        own_rows = pl.ds(12 * my_p, 12)
+        pltpu.make_async_copy(fb.at[t, own_rows], near.at[t, own_rows], nr.at[t]).start()
 
     def force_along_z(t):
         wait_for(near.at[t], nr.at[t])
-        total = near[t, 0]
-        for p in range(1, 32):
-            total = total + near[t, p]
-        own[t] = total
+        total = near[t, pl.ds(0, 24), :]
+        for p in range(1, 16):
+            total = total + near[t, pl.ds(24 * p, 24), :]
+        own[t] = total[:12] + total[12:]
 
         def along_z(d, carry):
             z, device = ring_z(me, d)
-            send(own.at[t, lax.rem(z, 4)], far.at[t, my_z], fs.at[t], fr.at[t], device)
+            send(own.at[t, pl.ds(3 * lax.rem(z, 4), 3)], far.at[t, pl.ds(3 * my_z, 3)], fs.at[t], fr.at[t], device)
             return carry
 
         lax.fori_loop(1, 8, along_z, 0)
-        pltpu.make_async_copy(own.at[t, me["zl"]], far.at[t, my_z], fr.at[t]).start()
+        own_rows = own.at[t, pl.ds(3 * me["zl"], 3)]
+        pltpu.make_async_copy(own_rows, far.at[t, pl.ds(3 * my_z, 3)], fr.at[t]).start()
 
     def force_out(t):
         wait_for(far.at[t], fr.at[t])
-        total = far[t, 0]
+        total = far[t, pl.ds(0, 3), :]
         for z in range(1, 8):
-            total = total + far[t, z]
+            total = total + far[t, pl.ds(3 * z, 3), :]
         cols = pl.ds(128 * t, 128)
         force[:, cols] = total * force_weight[:, cols]
 
+    for load in small:
+        load.wait()
     loads[0].wait()
     newton_but_last(0, matrix, approx, left, right, xr, xi)
     pl.semaphore_wait(barrier, 38)
     for t in range(T):
         newton_last(0, t, left, right, xr, xi, lin)
-        if t < 2:
+        if t < 1:
             z_forward(0, t)
     loads[1].wait()
     newton_but_last(1, matrix, approx, left, right, xr, xi)
     for t in range(T):
         newton_last(1, t, left, right, xr, xi, lin)
+        z_forward(1, t)
         if t < 2:
-            z_forward(1, t)
-    z_forward(0, 2)
-    z_forward(1, 2)
+            z_forward(0, t + 1)
+    for k in range(2):
+        for t in range(T):
+            for part in range(2):
+                green_out(k, t, part).start()
     plane_forward(0, 0)
     build_kernel()
-    plane_forward(0, 1)
     plane_forward(1, 0)
     convolve(0)
+    plane_forward(0, 1)
     plane_forward(1, 1)
-    convolve(1)
-    plane_forward(0, 2)
     z_back(0, 0)
     z_back(1, 0)
+    convolve(1)
     build_force_left()
-    plane_forward(1, 2)
+    plane_forward(0, 2)
     z_back(0, 1)
     z_back(1, 1)
+    plane_forward(1, 2)
     convolve(2)
     z_back(0, 2)
     z_back(1, 2)
@@ -328,12 +362,15 @@
 
     for t in range(T):
         for k in range(2):
+            for part in range(2):
+                green_out(k, t, part).wait()
+                sigma_out(k, t, part).wait()
             wait_for(zb.at[k, t, pl.ds(0, 7)], zs.at[k, t])
             wait_for(pb.at[k, t, :, pl.ds(0, 93)], ps.at[k, t])
             wait_for(rb.at[t, k, :, pl.ds(0, 93)], bs.at[t, k])
             wait_for(rb.at[t, k, pl.ds(0, 7)], ws.at[t, k])
-        wait_for(near.at[t, pl.ds(0, 31)], ns.at[t])
-        wait_for(far.at[t, pl.ds(0, 7)], fs.at[t])
+        wait_for(near.at[t, pl.ds(0, 372)], ns.at[t])
+        wait_for(far.at[t, pl.ds(0, 21)], fs.at[t])
 
 
 def step(matrix, approx, weight, shift, pairing, coupling, energy_weight, force_weight):
@@ -341,13 +378,23 @@
     return pl.pallas_call(
         step_kernel,
         out_shape=(
-            jax.ShapeDtypeStruct((T, 2, 2, B, 128), F32),
-            jax.ShapeDtypeStruct((2, T, 2, B, 128), F32),
+            jax.ShapeDtypeStruct((2, 1, 2, B, B), F32),
+            jax.ShapeDtypeStruct((2, 1, 2, B, B), F32),
             jax.ShapeDtypeStruct((3, B), F32),
         ),
-        in_specs=[pl.BlockSpec(memory_space=pl.ANY), VMEM, SMEM, SMEM, SMEM, VMEM, SMEM, VMEM],
-        out_specs=(VMEM, VMEM, VMEM),
+        in_specs=[pl.BlockSpec(memory_space=pltpu.HBM)] * 8,
+        out_specs=(pl.BlockSpec(memory_space=pltpu.HBM), pl.BlockSpec(memory_space=pltpu.HBM), VMEM),
         scratch_shapes=[
+            pltpu.VMEM((2, 2, B), F32),
+            pltpu.SMEM((4, 6), F32),
+            pltpu.SMEM((4, 6), jnp.int32),
+            pltpu.SMEM((4, 4), jnp.int32),
+            pltpu.VMEM((3, B), F32),
+            pltpu.SMEM((1,), F32),
+            pltpu.VMEM((3, B), F32),
+            dma((7,)),
+            pltpu.VMEM((2, T, 2, B, 128), F32),
+            pltpu.VMEM((T, 2, 2, B, 128), F32),
             pltpu.VMEM((2, 2, B, B), F32),
             pltpu.VMEM((2 * B, 6 * B), BF16),
             pltpu.VMEM((6 * B, 2 * B), BF16),
@@ -360,12 +407,13 @@
             pltpu.VMEM((512, 1536), BF16),
             pltpu.VMEM((4, 128, 128), F32),
             pltpu.VMEM((1536, 384), BF16),
-            pltpu.VMEM((B, 12 * B), BF16),
-            pltpu.VMEM((12 * B, 128), BF16),
-            pltpu.VMEM((T, 4, 96, 128), F32),
-            pltpu.VMEM((T, 32, 4, 3, 128), F32),
-            pltpu.VMEM((T, 4, 3, 128), F32),
-            pltpu.VMEM((T, 8, 3, 128), F32),
+            pltpu.VMEM((2, B, 6 * B), BF16),
+            pltpu.VMEM((6 * B, 128), BF16),
+            pltpu.VMEM((B, 128), F32),
+            pltpu.VMEM((T, B, 128), F32),
+            pltpu.VMEM((T, B, 128), F32),
+            pltpu.VMEM((T, 12, 128), F32),
+            pltpu.VMEM((T, 24, 128), F32),
             dma((2,)),
             dma((2, T)), dma((2, T)),
             dma((2, T)), dma((2, T)),
@@ -373,48 +421,67 @@
             dma((T, 2)), dma((T, 2)),
             dma((T,)), dma((T,)),
             dma((T,)), dma((T,)),
+            dma((2, T, 2)), dma((2, T, 2)),
         ],
         compiler_params=pltpu.CompilerParams(
-            collective_id=1, has_side_effects=True, vmem_limit_bytes=52 << 20
+            collective_id=1, has_side_effects=True, vmem_limit_bytes=67043328
         ),
         name="step",
     )(matrix, approx, weight, shift, pairing, coupling, energy_weight, force_weight)
 
 
-def layout_kernel(raw, lin, f_in, green, sigma, f_out):
-    part = pl.program_id(0)
-    k = pl.program_id(1)
-    for t in range(T):
-        cols = pl.ds(128 * t, 128)
-        green[0, 0, 0, :, cols] = lin[k, t, part]
-        sigma[0, 0, 0, :, cols] = raw[t, k, part]
-    f_out[...] = f_in[...]
-
-
-def final_layouts(raw, lin, force):
-    block = pl.BlockSpec((1, 1, 1, B, B), lambda part, k: (part, 0, k, 0, 0))
+def copy_kernel(green, sigma, force, green_out, sigma_out, force_out, held, arrived, left):
+    moves = []
+    for n, (src, dst) in enumerate(((green, green_out), (sigma, sigma_out))):
+        for part in range(2):
+            for k in range(2):
+                for h in range(CUT):
+                    rows = pl.ds(h * (B // CUT), B // CUT)
+                    m = len(moves)
+                    place = held.at[n, part, k, rows]
+                    moves.append((
+                        pltpu.make_async_copy(src.at[part, 0, k, rows], place, arrived.at[m]),
+                        pltpu.make_async_copy(place, dst.at[part, 0, k, rows], left.at[m]),
+                    ))
+    for inward, _ in moves:
+        inward.start()
+    force_out[...] = force[...]
+    for inward, outward in moves:
+        inward.wait()
+        outward.start()
+    for _, outward in moves:
+        outward.wait()
+
+
+CUT = 2
+
+
+def final_copies(green, sigma, force):
+    hbm = pl.BlockSpec(memory_space=pltpu.HBM)
+    large = jax.ShapeDtypeStruct((2, 1, 2, B, B), F32)
     return pl.pallas_call(
-        layout_kernel,
-        grid=(2, 2),
-        out_shape=(
-            jax.ShapeDtypeStruct((2, 1, 2, B, B), F32),
-            jax.ShapeDtypeStruct((2, 1, 2, B, B), F32),
-            jax.ShapeDtypeStruct((3, B), F32),
-        ),
-        in_specs=[VMEM, VMEM, VMEM],
-        out_specs=(block, block, pl.BlockSpec((3, B), lambda part, k: (0, 0))),
-        name="layouts",
-    )(raw, lin, force)
+        copy_kernel,
+        out_shape=(large, large, jax.ShapeDtypeStruct((3, B), F32)),
+        in_specs=[hbm, hbm, VMEM],
+        out_specs=(hbm, hbm, VMEM),
+        scratch_shapes=[
+            pltpu.VMEM((2, 2, 2, B, B), F32),
+            pltpu.SemaphoreType.DMA((8 * CUT,)),
+            pltpu.SemaphoreType.DMA((8 * CUT,)),
+        ],
+        compiler_params=pltpu.CompilerParams(vmem_limit_bytes=67043328),
+        name="copies",
+    )(green, sigma, force)
 
 
 def per_device(
     system_matrix, approx_inverse, mode_weight, phonon_shift, pairing, coupling, energy_weight, force_weight
 ):
-    raw, lin, force = step(
+    green, sigma, force = step(
         system_matrix, approx_inverse.reshape(2, 2, B), mode_weight, phonon_shift, pairing, coupling,
         energy_weight, force_weight,
     )
-    return final_layouts(raw, lin, force)
+    return final_copies(green, sigma, force)
 
 
 def solution(mesh):

time: 154 us -> 141 us (0.916)
  Pallas kernels: 148 us -> 139 us
  local copies, waits for them, and re-layouts: 4.7 us -> 0 us
    pallas_call x2, Pallas kernels: 148 us -> 139 us  [the longest x1 133 us: step(): pl.pallas_call(step_kernel, out_shape=(jax.ShapeDtypeStruct((2, 1, 2, B,...]
    unnamed x14 -> x0, local copies, waits for them, and re-layouts: 4.7 us -> none
where the time goes in v2:
time: 141 us
  Pallas kernels  139 us (99%)
  between operations  1.45 us (1%)
    pallas_call x1, Pallas kernels, step(): pl.pallas_call(step_kernel, out_shape=(jax.ShapeDtypeStruct((2, 1, 2, B,...  133 us
    pallas_call x1, Pallas kernels, final_copies(): pl.pallas_call(copy_kernel, out_shape=(large, large, jax.ShapeDtypeStruct...  5.66 us

profile of v2, /device:TPU:1, one launch (start us, length us, event | category | flops | bytes accessed | tf_op | source)
XLA Modules:
  0.0 140.5 jit_solution(18348159943479883623)
XLA Ops:
  1.3 133.4 %step.1 = (f32[2,1,2,384,384]{4,3,2,1,0:T(8,128)}, f32[2,1,2,384,384]{4,3,2,1,0:T(8,128)}, f32[3,384]{1,0:T(4,128)}) custom-call(f32[2,1,2,384,384]{4,3,2,1,0:T(8,128)} %matrix_hbm.1, f32[2,2,384]{2,1,0:T(2,128)} %bitcast.1, f32[4,6]{1,0:T(4,128)} %weight_hbm.1, s32[4,6]{1,0:T(4,128)} %shift_hbm.1, s32[4,4]{1,0:T(4,128)} %pairing_hbm.1, ...), custom_call_target="tpu_custom_call" | custom-call | tf_op jit(solution)/shard_map/step/pallas_call | solution.py:378
  134.7 5.7 %copies.1 = (f32[2,1,2,384,384]{4,3,2,1,0:T(8,128)}, f32[2,1,2,384,384]{4,3,2,1,0:T(8,128)}, f32[3,384]{1,0:T(4,128)}) custom-call(f32[2,1,2,384,384]{4,3,2,1,0:T(8,128)} %get-tuple-element.6.green, f32[2,1,2,384,384]{4,3,2,1,0:T(8,128)} %get-tuple-element.7.sigma, f32[3,384]{1,0:T(4,128)} %get-tuple-element.8.force), custom_call_target="tpu_custom_call" | custom-call | tf_op jit(solution)/shard_map/copies/pallas_call | solution.py:462

commit v3 on v2

--- a/solution.py
+++ b/solution.py
@@ -97,15 +97,22 @@
     return {a: lax.axis_index(a) for a in AXES}
 
 
-def ring_z(me, d):
-    z = lax.rem(me["zh"] * 4 + me["zl"] + d, 8)
+def ring_z(me, n):
+    side = (2 * lax.rem(n, 2) - 1) * (1 - 2 * me["c"])
+    z = lax.rem(me["zh"] * 4 + me["zl"] + 4 + side * (n // 2), 8)
     return z, (lax.rem(z, 4), me["x"], me["y"], me["c"], z // 4)
 
 
+def far_first(n):
+    late = n // 2
+    return (1 - late) * (2 - n) + late * lax.rem(n + 1, 4)
+
+
 def plane(me, i):
-    x = lax.rem(me["x"] + i // 8, 4)
-    y = lax.rem(me["y"] + lax.rem(i // 2, 4), 4)
-    c = lax.rem(me["c"] + lax.rem(i, 2), 2)
+    n = i - 1
+    x = lax.rem(me["x"] + far_first(n // 8), 4)
+    y = lax.rem(me["y"] + far_first(lax.rem(n // 2, 4)), 4)
+    c = lax.rem(me["c"] + 1 - lax.rem(n, 2), 2)
     return (x * 4 + y) * 2 + c, (me["zl"], x, y, c, me["zh"])
 
 
@@ -286,7 +293,7 @@
             send(fb.at[t, pl.ds(12 * p, 12)], near.at[t, pl.ds(12 * my_p, 12)], ns.at[t], nr.at[t], device)
             return carry
 
-        lax.fori_loop(1, 32, in_plane, 0)
+        lax.fori_loop(1, 32, in_plane, 0, unroll=True)
         own_rows = pl.ds(12 * my_p, 12)
         pltpu.make_async_copy(fb.at[t, own_rows], near.at[t, own_rows], nr.at[t]).start()
 
@@ -302,7 +309,7 @@
             send(own.at[t, pl.ds(3 * lax.rem(z, 4), 3)], far.at[t, pl.ds(3 * my_z, 3)], fs.at[t], fr.at[t], device)
             return carry
 
-        lax.fori_loop(1, 8, along_z, 0)
+        lax.fori_loop(1, 8, along_z, 0, unroll=True)
         own_rows = own.at[t, pl.ds(3 * me["zl"], 3)]
         pltpu.make_async_copy(own_rows, far.at[t, pl.ds(3 * my_z, 3)], fr.at[t]).start()
 

time: 141 us -> 139 us (0.986)
  no operation moved by 1% of the time
where the time goes in v3:
time: 139 us
  Pallas kernels  138 us (99%)
  between operations  1.45 us (1%)
    pallas_call x1, Pallas kernels, step(): pl.pallas_call(step_kernel, out_shape=(jax.ShapeDtypeStruct((2, 1, 2, B,...  132 us
    pallas_call x1, Pallas kernels, final_copies(): pl.pallas_call(copy_kernel, out_shape=(large, large, jax.ShapeDtypeStruct...  5.66 us

profile of v3, /device:TPU:1, one launch (start us, length us, event | category | flops | bytes accessed | tf_op | source)
XLA Modules:
  0.0 139.3 jit_solution(18159913126429597673)
XLA Ops:
  1.3 132.2 %step.1 = (f32[2,1,2,384,384]{4,3,2,1,0:T(8,128)}, f32[2,1,2,384,384]{4,3,2,1,0:T(8,128)}, f32[3,384]{1,0:T(4,128)}) custom-call(f32[2,1,2,384,384]{4,3,2,1,0:T(8,128)} %matrix_hbm.1, f32[2,2,384]{2,1,0:T(2,128)} %bitcast.1, f32[4,6]{1,0:T(4,128)} %weight_hbm.1, s32[4,6]{1,0:T(4,128)} %shift_hbm.1, s32[4,4]{1,0:T(4,128)} %pairing_hbm.1, ...), custom_call_target="tpu_custom_call" | custom-call | tf_op jit(solution)/shard_map/step/pallas_call | solution.py:385
  133.5 5.7 %copies.1 = (f32[2,1,2,384,384]{4,3,2,1,0:T(8,128)}, f32[2,1,2,384,384]{4,3,2,1,0:T(8,128)}, f32[3,384]{1,0:T(4,128)}) custom-call(f32[2,1,2,384,384]{4,3,2,1,0:T(8,128)} %get-tuple-element.6.green, f32[2,1,2,384,384]{4,3,2,1,0:T(8,128)} %get-tuple-element.7.sigma, f32[3,384]{1,0:T(4,128)} %get-tuple-element.8.force), custom_call_target="tpu_custom_call" | custom-call | tf_op jit(solution)/shard_map/copies/pallas_call | solution.py:469
